TPU v7x, 32 devices: a whole 2x2x4 slice. The times are simulated.
32 devices in a mesh: groups: 2 (over y), space: 16 (over z, x, core).
Axes of the slice: x: 2, y: 2, z: 4, core: 2. Of those that a mesh axis runs over, the one named last changes fastest.
Arguments:
- modes: float32 [4, 128, 32, 64], P('groups', None, 'space'), parts along dimension 0, may hold values from -6 to 6
- cell_weight: float32 [32, 128], P('space', 'groups'), parts along dimension 1, may hold values from 0.5 to 2
- seeds: int32 [256], P(('groups', 'space')), parts along dimension 0, may hold values from 0 to 255
- coeff_table: float32 [256, 128], replicated, may hold values from -6 to 6
- force_table: float32 [256, 128], replicated, may hold values from -6 to 6
- visc_table: float32 [256], replicated, may hold values from 0.02 to 0.2
Outputs:
- coefficients: float32 [256, 128], P(('groups', 'space')), parts along dimension 0
There are 2 independent parts, one for each index of `groups`. A program takes and returns all parts, laid end to end along the dimension named above; an argument that names none is the same for every part. Nothing has to cross between parts.
All inputs are finite; a program needn't handle non-finite values.
Results may differ from a plain program's by a relative error of at most 0.00013.
Values sent between devices are 32-bit elements; how exact they have to be, the bound alone decides.
A program may use at most 64 MiB of HBM per device.

v0:
```python
import functools

import jax
import jax.numpy as jnp
from jax import lax
from jax.experimental import pallas as pl
from jax.experimental.pallas import tpu as pltpu
from jax.sharding import PartitionSpec as P

TIME_STEP = 0.5

MESH = pl.DeviceIdType.MESH

ROWS = ((1,), (0,))
LANES = ((1,), (1,))


def split(x):
    high = x.astype(jnp.bfloat16)
    return high, (x - high.astype(jnp.float32)).astype(jnp.bfloat16)


def product(a, b, contract):
    return lax.dot_general(a, b, (contract, ((), ())), preferred_element_type=jnp.float32)


BLOCK = 4

HALVES = 2


def product_3(a, b, contract):
    rows = a[0].shape[0]
    both = product(jnp.concatenate(a, axis=0), b[0], contract)
    return (product(a[0], b[1], contract) + both[rows:]) + both[:rows]


def kernel(
    n,
    across,
    modes_hbm,
    weight_hbm,
    seeds_hbm,
    visc_hbm,
    coeff_hbm,
    force_hbm,
    out_ref,
    slabs,
    weights,
    seeds_ref,
    visc_ref,
    coeff_ref,
    force_ref,
    seed_rows,
    spots,
    high,
    low,
    wide_high,
    wide_low,
    partial,
    landed,
    group_sum,
    group_landed,
    group_coeffs,
    group_force,
    last,
    last_landed,
    load_sem,
    slab_send,
    slab_recv,
    send_sem,
    recv_sem,
):
    me = lax.axis_index("space")
    blocks = n // BLOCK
    block, seat = me // BLOCK, lax.rem(me, BLOCK)
    base = me - seat
    own = seeds_hbm.shape[0]
    cells = modes_hbm.shape[1]
    mode_count = modes_hbm.shape[2]
    slab = cells // across
    params = coeff_ref.shape[0]
    total = own * n
    group = own * blocks
    half = blocks // HALVES
    partner = me + 1 - 2 * lax.rem(seat, 2)
    mirror = base + BLOCK - 1 - seat
    place = seat + 1
    high_end = seat // (BLOCK - 1)
    outer = high_end * (BLOCK + 1)
    beyond = lax.rem(me + n - 1 + 2 * high_end, n)
    at_end = (seat == 0) | (seat == BLOCK - 1)
    inside = jnp.logical_not(at_end)

    barrier = pltpu.get_barrier_semaphore()

    @pl.loop(1, n)
    def _(d):
        pl.semaphore_signal(
            barrier, inc=1, device_id={"space": lax.rem(me + d, n)}, device_id_type=MESH
        )

    loads = [
        pltpu.make_async_copy(source, target, load_sem.at[i])
        for i, (source, target) in enumerate(
            (
                (seeds_hbm, seeds_ref),
                (modes_hbm, slabs.at[:, place]),
                (weight_hbm, weights.at[seat]),
                (coeff_hbm, coeff_ref),
                (force_hbm, force_ref),
                (visc_hbm, visc_ref),
            )
        )
    ]
    for load in loads:
        load.start()
    loads[0].wait()
    lane = lax.broadcasted_iota(jnp.int32, (1, total), 1)
    row = jnp.zeros((1, total), jnp.int32)
    for r in range(own):
        row = jnp.where(lane == me * own + r, seeds_ref[r], row)
    seed_rows[0] = row
    loads[1].wait()
    loads[2].wait()

    pl.semaphore_wait(barrier, n - 1)

    def spread(phase, count, peer_of, source, target):
        @pl.loop(1, count)
        def _(d):
            peer = peer_of(d)
            pltpu.make_async_remote_copy(
                src_ref=source(peer),
                dst_ref=target(d),
                send_sem=send_sem.at[phase],
                recv_sem=recv_sem.at[phase],
                device_id={"space": peer},
                device_id_type=MESH,
            ).start()

    def anyone(d):
        return lax.rem(me + d, n)

    def in_block(d):
        return base + lax.rem(seat + d, BLOCK)

    def in_group(d):
        return lax.rem(me + BLOCK * d, n)

    def whole(phase, ref):
        return pltpu.make_async_remote_copy(
            src_ref=ref,
            dst_ref=ref,
            send_sem=send_sem.at[phase],
            recv_sem=recv_sem.at[phase],
            device_id={"space": partner},
            device_id_type=MESH,
        )

    def slab_copy(i, source, target, peer):
        return pltpu.make_async_remote_copy(
            src_ref=slabs.at[:, source],
            dst_ref=slabs.at[:, target],
            send_sem=slab_send.at[i],
            recv_sem=slab_recv.at[target],
            device_id={"space": peer},
            device_id_type=MESH,
        )

    def arrived(slot):
        slab_copy(0, slot, slot, partner).wait_recv()

    to_beyond = slab_copy(0, place, BLOCK + 1 - outer, beyond)
    to_mirror = slab_copy(1, place, place, mirror)
    to_partner = slab_copy(2, place, place, partner)

    spread(0, n, anyone, lambda peer: seed_rows.at[0], lambda d: seed_rows.at[d])

    @pl.when(at_end)
    def _():
        to_beyond.start()

    @pl.when(inside)
    def _():
        to_mirror.start()

    to_partner.start()
    spread(1, BLOCK, in_block, lambda peer: weights.at[seat], lambda d: weights.at[seat])

    def lateral(f, shift):
        layers = [
            pltpu.roll(f[s * across : (s + 1) * across], shift % across, 0)
            for s in range(f.shape[0] // across)
        ]
        return jnp.concatenate(layers, axis=0)

    def across_slope(f):
        return (
            lateral(f, 2) - 8.0 * lateral(f, 1) + 8.0 * lateral(f, -1) - lateral(f, -2)
        ) / 12.0

    def along_slope(f):
        width = f.shape[0] - 2 * cells
        g = [
            f[cells + shift * across : cells + width + shift * across] for shift in (-2, -1, 1, 2)
        ]
        return (g[0] - 8.0 * g[1] + 8.0 * g[2] - g[3]) / 12.0

    def keep(q, x):
        high[q * cells : (q + 1) * cells, :], low[q * cells : (q + 1) * cells, :] = split(x)

    for a in range(2):
        f = slabs[a, place]
        keep(a, f)
        keep(2 + a, across_slope(f))
    for load in loads[3:]:
        load.wait()
    table = split(coeff_ref[...])

    seed_bytes = whole(0, seed_rows.at[pl.ds(1, n - 1)])
    seed_bytes.wait_recv()
    seeds = jnp.sum(seed_rows[...], axis=0)
    spot = jnp.broadcast_to(seeds.astype(jnp.float32), (128, total)).T
    spots[...] = spot.reshape(blocks, BLOCK, own, 128)

    def choose(spot):
        spot = jnp.concatenate([spot] * (params // 128), axis=1)
        chosen = spot == lax.broadcasted_iota(jnp.int32, spot.shape, 1).astype(jnp.float32)
        viscosity = jnp.sum(jnp.where(chosen, visc_ref[...], 0.0), axis=1, keepdims=True)
        return chosen.astype(jnp.float32), viscosity

    chosen, viscosity = choose(spot)
    chosen = chosen.astype(jnp.bfloat16)
    now = [product(chosen, half, ROWS).astype(jnp.bfloat16) for half in table]

    def scale_of(held):
        parts = [w[s : s + 1, :] for w in held for s in range(slab)]
        return jnp.concatenate(parts, axis=1) / (cells * n)

    def pieces(now, high, low, start, count):
        size = high.shape[0] // 6
        rows = slice(start * size, (start + count) * size)
        gathered = product_3(now, (high[rows, :], low[rows, :]), LANES)
        return [gathered[:, q * size : (q + 1) * size] for q in range(count)]

    def advance(part, basis, scale, viscosity):
        fields = [scale * (part[0] * part[4 + a] + part[1] * part[2 + a]) for a in range(2)]
        damped = viscosity * scale
        fields += [damped * part[q] for q in range(2, 6)]
        return product_3(split(jnp.concatenate(fields, axis=1)), basis, ROWS)

    part = pieces(now, high, low, 0, 4)
    arrived(seat)
    arrived(seat + 2)

    edge_partner = slab_copy(3, outer, outer, partner)
    edge_mirror = slab_copy(4, outer, outer, mirror)
    inner_partner = slab_copy(3, BLOCK - seat, BLOCK - seat, partner)

    @pl.when(at_end)
    def _():
        to_mirror.start()
        edge_partner.start()

    @pl.when(inside)
    def _():
        inner_partner.start()

    for a in range(2):
        f = slabs[a, pl.ds(seat, 3)].reshape(3 * cells, mode_count)
        keep(4 + a, along_slope(f))
    part += pieces(now, high, low, 4, 2)
    near_scale = scale_of([weights[seat]])
    for h in range(HALVES):
        rows = slice(h * total // HALVES, (h + 1) * total // HALVES)
        change = advance(
            [p[rows] for p in part], (high[...], low[...]), near_scale, viscosity[rows]
        )
        partial[h * half : (h + 1) * half] = change.reshape(half, BLOCK, own, mode_count)
        spread(
            2 + h,
            BLOCK,
            in_block,
            lambda peer: partial.at[pl.ds(h * half, half), peer - base],
            lambda d: landed.at[h, d - 1],
        )

    @pl.when(at_end)
    def _():
        edge_mirror.start()

    chosen, viscosity = choose(spots[:, seat].reshape(group, 128))
    coeffs = lax.dot(chosen, coeff_ref[...], precision=lax.Precision.HIGHEST)
    forcing = lax.dot(chosen, force_ref[...], precision=lax.Precision.HIGHEST)
    weight_bytes = whole(1, weights.at[pl.ds(0, BLOCK - 1)])
    weight_bytes.wait_recv()
    scale = scale_of([weights[s] for s in range(BLOCK)])

    sums, block_bytes, group_bytes = [], [], []
    for h in range(HALVES):
        block_bytes.append(whole(2 + h, landed.at[h]))
        block_bytes[h].wait_recv()
        summed = partial[h * half : (h + 1) * half, seat] + jnp.sum(landed[h], axis=0)
        sums.append(summed.reshape(own * half, mode_count))
        group_sum[h] = sums[h]
        spread(
            2 + HALVES + h,
            blocks,
            in_group,
            lambda peer: group_sum.at[h],
            lambda d: group_landed.at[h, d - 1],
        )

    other = BLOCK - seat
    late_1 = slab_copy(5, other, other, partner)
    late_2 = slab_copy(6, BLOCK + 1 - outer, BLOCK + 1 - outer, partner)

    @pl.when(at_end)
    def _():
        arrived(other)
        late_1.start()
        arrived(BLOCK + 1 - outer)
        late_2.start()
        arrived(3 - high_end)

    @pl.when(inside)
    def _():
        for k in range(3):
            arrived(lax.rem(seat + 3 + k, BLOCK + 2))

    size = BLOCK * cells

    def keep_wide(q, x):
        wide_high[q * size : (q + 1) * size, :], wide_low[q * size : (q + 1) * size, :] = split(x)

    for a in range(2):
        f = slabs[a].reshape((BLOCK + 2) * cells, mode_count)
        middle = f[cells : cells + size]
        keep_wide(a, middle)
        keep_wide(2 + a, across_slope(middle))
        keep_wide(4 + a, along_slope(f))

    for h in range(HALVES):
        group_bytes.append(whole(2 + HALVES + h, group_landed.at[h]))
        group_bytes[h].wait_recv()
        sums[h] = sums[h] + jnp.sum(group_landed[h], axis=0)
    change = jnp.concatenate(sums, axis=0)
    coeffs = coeffs + TIME_STEP * (forcing - change)
    group_coeffs[...] = coeffs.reshape(blocks, own, mode_count)
    group_force[...] = forcing.reshape(blocks, own, mode_count)
    part = pieces(split(coeffs), wide_high, wide_low, 0, 6)
    change = advance(part, (wide_high[...], wide_low[...]), scale, viscosity)
    last[...] = change.reshape(blocks, own, mode_count)
    spread(
        2 + 2 * HALVES, blocks, in_group, lambda peer: last.at[peer // BLOCK], lambda d: last_landed.at[d - 1]
    )
    last_bytes = whole(2 + 2 * HALVES, last_landed)
    last_bytes.wait_recv()
    change = last[block] + jnp.sum(last_landed[...], axis=0)
    out_ref[...] = group_coeffs[block] + TIME_STEP * (group_force[block] - change)

    to_mirror.wait_send()
    to_partner.wait_send()

    @pl.when(at_end)
    def _():
        for copy in (to_beyond, edge_partner, edge_mirror, late_1, late_2):
            copy.wait_send()

    @pl.when(inside)
    def _():
        inner_partner.wait_send()

    for sent in (seed_bytes, weight_bytes, *block_bytes, *group_bytes, last_bytes):
        sent.wait_send()


def shards(modes, cell_weight, seeds, coeff_table, force_table, visc_table):
    components, mode_count, slab_cells, across = modes.shape
    n = lax.axis_size("space")
    blocks = n // BLOCK
    cells = slab_cells * across
    own = seeds.shape[0]
    total = own * n
    params = coeff_table.shape[0]
    f32, bf16 = jnp.float32, jnp.bfloat16
    return pl.pallas_call(
        functools.partial(kernel, n, across),
        out_shape=pltpu.VMEM((own, mode_count), f32),
        in_specs=[pl.BlockSpec(memory_space=pl.ANY)] * 6,
        out_specs=pl.BlockSpec(memory_space=pltpu.VMEM),
        scratch_shapes=[
            pltpu.VMEM((components, BLOCK + 2, cells, mode_count), f32),
            pltpu.VMEM((BLOCK, slab_cells, across), f32),
            pltpu.SMEM((own,), jnp.int32),
            pltpu.VMEM((1, params), f32),
            pltpu.VMEM((params, mode_count), f32),
            pltpu.VMEM((params, mode_count), f32),
            pltpu.VMEM((n, 1, total), jnp.int32),
            pltpu.VMEM((blocks, BLOCK, own, 128), f32),
            pltpu.VMEM((6 * cells, mode_count), bf16),
            pltpu.VMEM((6 * cells, mode_count), bf16),
            pltpu.VMEM((6 * BLOCK * cells, mode_count), bf16),
            pltpu.VMEM((6 * BLOCK * cells, mode_count), bf16),
            pltpu.VMEM((blocks, BLOCK, own, mode_count), f32),
            pltpu.VMEM((HALVES, BLOCK - 1, blocks // HALVES, own, mode_count), f32),
            pltpu.VMEM((HALVES, own * blocks // HALVES, mode_count), f32),
            pltpu.VMEM((HALVES, blocks - 1, own * blocks // HALVES, mode_count), f32),
            pltpu.VMEM((blocks, own, mode_count), f32),
            pltpu.VMEM((blocks, own, mode_count), f32),
            pltpu.VMEM((blocks, own, mode_count), f32),
            pltpu.VMEM((blocks - 1, own, mode_count), f32),
            pltpu.SemaphoreType.DMA((6,)),
            pltpu.SemaphoreType.DMA((7,)),
            pltpu.SemaphoreType.DMA((BLOCK + 2,)),
            pltpu.SemaphoreType.DMA((3 + 2 * HALVES,)),
            pltpu.SemaphoreType.DMA((3 + 2 * HALVES,)),
        ],
        compiler_params=pltpu.CompilerParams(collective_id=0, has_side_effects=True),
    )(
        modes.transpose(0, 2, 3, 1).reshape(components, cells, mode_count),
        cell_weight,
        seeds,
        visc_table.reshape(1, -1),
        coeff_table,
        force_table,
    )


def solution(mesh):
    placed = (
        P("groups", None, "space", None),
        P("space", "groups"),
        P(("groups", "space")),
        P(),
        P(),
        P(),
    )
    return jax.shard_map(
        shards, mesh=mesh, in_specs=placed, out_specs=P(("groups", "space"), None), check_vma=False
    )
```

profile of v0, /device:TPU:0, one launch (start us, length us, event | category | flops | bytes accessed | tf_op | source)
XLA Modules:
  0.0 23.9 jit_solution(13287007917440684094)
XLA Ops:
  0.0 23.3 %shard_map.64 = f32[8,128]{1,0:T(8,128)S(1)} custom-call(f32[2,128,128]{2,1,0:T(8,128)} %bitcast.4, f32[2,64]{1,0:T(2,128)} %weight_hbm.1, s32[8]{0:T(128)} %seeds_hbm.1, f32[1,256]{1,0:T(1,128)} %bitcast.5, f32[256,128]{1,0:T(8,128)} %coeff_hbm.1, f32[256,128]{1,0:T(8,128)} %force_hbm.1), custom_call_target="tpu_custom_call" | custom-call | tf_op jit(solution)/shard_map/pallas_call | solution.py:388
  23.3 0.6 %copy.8 = f32[8,128]{1,0:T(8,128)} copy(f32[8,128]{1,0:T(8,128)S(1)} %shard_map.64) | data formatting | bytes 8192
where the time goes:
time: 24 us; the launch traced here: 23.9 us
  Pallas kernels  23.3 us (97%)
  local copies, waits for them, and re-layouts  0.6 us (2%)
    pallas_call x1, Pallas kernels, shards(): pl.pallas_call(functools.partial(kernel, n, across), out_shape=pltpu.VMEM...  23.3 us
    unnamed x1, local copies, waits for them, and re-layouts  0.6 us

commit v1 on v0

v1 whole, which is shorter than its diff:
```python
import functools

import jax
import jax.numpy as jnp
from jax import lax
from jax.experimental import pallas as pl
from jax.experimental.pallas import tpu as pltpu
from jax.sharding import PartitionSpec as P

TIME_STEP = 0.5

MESH = pl.DeviceIdType.MESH

ROWS = ((1,), (0,))
LANES = ((1,), (1,))

ROW = 4

TAIL = 8


def product(a, b, contract):
    return lax.dot_general(a, b, (contract, ((), ())), preferred_element_type=jnp.float32)


def split(x, count):
    terms = []
    for _ in range(count):
        terms.append(x.astype(jnp.bfloat16))
        x = x - terms[-1].astype(jnp.float32)
    return terms


def stack(x, count):
    terms = []
    for _ in range(count):
        terms.append(x.astype(jnp.bfloat16).astype(jnp.float32))
        x = x - terms[-1]
    return jnp.concatenate(terms, axis=0).astype(jnp.bfloat16)


def kernel(
    n,
    across,
    modes_hbm,
    weight_hbm,
    seeds_hbm,
    visc_hbm,
    coeff_hbm,
    force_hbm,
    out_ref,
    slabs,
    high,
    mid,
    low,
    speeds,
    weight_ref,
    seeds_ref,
    visc_ref,
    coeff_ref,
    force_ref,
    picks,
    partial,
    landed,
    now_ref,
    push_ref,
    last,
    last_landed,
    load_sem,
    send_sem,
    recv_sem,
    small_sem,
    ok,
):
    me = lax.axis_index("space")
    rows = n // ROW
    row, seat = me // ROW, lax.rem(me, ROW)
    base = me - seat
    side, core = seat // 2, lax.rem(seat, 2)
    own = seeds_hbm.shape[0]
    depth = modes_hbm.shape[0]
    cells = depth // 2
    layers = weight_hbm.shape[0]
    params = coeff_hbm.shape[0]
    total = own * rows
    partner = me + 1 - 2 * core
    mirror = me + 2 - 4 * side
    above = lax.rem(row + 1, rows) * ROW
    below = lax.rem(row + rows - 1, rows) * ROW
    first, final = seat == 0, seat == ROW - 1
    place = seat + 1

    loads = [
        pltpu.make_async_copy(source, target, load_sem.at[i])
        for i, (source, target) in enumerate(
            (
                (modes_hbm, slabs.at[place, pl.ds(0, depth)]),
                (weight_hbm, weight_ref),
                (seeds_hbm, seeds_ref),
                (coeff_hbm, coeff_ref),
                (force_hbm, force_ref),
                (visc_hbm, visc_ref),
            )
        )
    ]
    for load in loads:
        load.start()

    barrier = pltpu.get_barrier_semaphore()

    def tell(peer):
        pl.semaphore_signal(barrier, inc=1, device_id={"space": peer}, device_id_type=MESH)

    def in_column(d):
        return lax.rem(me + ROW * d, n)

    bottom, top = row == 0, row == rows - 1

    @pl.when(core == 0)
    def _():
        tell(partner)

    @pl.when(side == 0)
    def _():
        tell(mirror)

    @pl.when(first & bottom)
    def _():
        tell(below + ROW - 1)
        tell(below + 1)

    @pl.when((seat == 2) & bottom)
    def _():
        tell(below + ROW - 1)

    @pl.when((seat == 1) & jnp.logical_not(top))
    def _():
        tell(above)

    @pl.when(final & jnp.logical_not(top))
    def _():
        tell(above)
        tell(above + 2)

    @pl.loop(row + 1, rows)
    def _(r):
        tell(r * ROW + seat)

    def answer(at, peer):
        pl.semaphore_signal(ok.at[at], inc=1, device_id={"space": peer}, device_id_type=MESH)

    def send(kind, source, target, peer):
        pltpu.make_async_remote_copy(
            src_ref=slabs.at[source],
            dst_ref=slabs.at[target],
            send_sem=send_sem.at[kind],
            recv_sem=recv_sem.at[target],
            device_id={"space": peer},
            device_id_type=MESH,
        ).start()

    def waiting(ref, send_at, recv_at):
        return pltpu.make_async_remote_copy(
            src_ref=ref,
            dst_ref=ref,
            send_sem=send_at,
            recv_sem=recv_at,
            device_id={"space": partner},
            device_id_type=MESH,
        )

    def arrived(slot):
        waiting(slabs.at[slot], send_sem.at[0], recv_sem.at[slot]).wait_recv()

    def spread(phase, source, target):
        @pl.loop(1, rows)
        def _(d):
            pltpu.make_async_remote_copy(
                src_ref=source(lax.rem(row + d, rows)),
                dst_ref=target(d),
                send_sem=send_sem.at[2 + phase],
                recv_sem=small_sem.at[phase],
                device_id={"space": in_column(d)},
                device_id_type=MESH,
            ).start()

    loads[2].wait()
    row_of = lax.broadcasted_iota(jnp.int32, (own, 128), 0)
    picked = jnp.zeros((own, 128), jnp.int32)
    for r in range(own):
        picked = jnp.where(row_of == r, seeds_ref[r], picked)
    picks[row] = picked
    loads[1].wait()
    weight = [weight_ref[s : s + 1, :] for s in range(layers)]
    slabs[place, depth : depth + 1, :] = jnp.concatenate(weight, axis=1) / (cells * n)
    loads[0].wait()

    def seeds_to(r):
        pltpu.make_async_remote_copy(
            src_ref=picks.at[row],
            dst_ref=picks.at[row],
            send_sem=send_sem.at[2],
            recv_sem=small_sem.at[0],
            device_id={"space": r * ROW + seat},
            device_id_type=MESH,
        ).start()

    def outer_down():
        send(1, place, ROW + 1, below + 1)
        send(1, place, ROW + 1, below + ROW - 1)

    def outer_up():
        send(1, place, 0, above)
        send(1, place, 0, above + 2)

    lower = core + side + row
    lower += jnp.where(jnp.logical_not(bottom) & first, 2, 0)
    lower += jnp.where(jnp.logical_not(bottom) & (seat == 2), 1, 0)
    lower += jnp.where(top & final, 2, 0) + jnp.where(top & (seat == 1), 1, 0)
    @pl.when(lower > 0)
    def _():
        pl.semaphore_wait(barrier, lower)

    @pl.when(core == 1)
    def _():
        answer(0, partner)
        send(0, place, place, partner)

    @pl.when(side == 1)
    def _():
        answer(1, mirror)
        send(0, place, place, mirror)

    @pl.when(top & final)
    def _():
        answer(2, above)

    @pl.when(top & (seat == 1))
    def _():
        answer(2, above)

    @pl.when(jnp.logical_not(bottom) & (first | (seat == 2)))
    def _():
        answer(2, below + ROW - 1)

    @pl.loop(0, row)
    def _(r):
        answer(3, r * ROW + seat)
        seeds_to(r)

    @pl.when(first & jnp.logical_not(bottom))
    def _():
        outer_down()

    @pl.when(final & top)
    def _():
        outer_up()

    @pl.when(core == 0)
    def _():
        pl.semaphore_wait(ok.at[0], 1)
        send(0, place, place, partner)

    @pl.when(side == 0)
    def _():
        pl.semaphore_wait(ok.at[1], 1)
        send(0, place, place, mirror)

    @pl.when(final & jnp.logical_not(top))
    def _():
        pl.semaphore_wait(ok.at[2], 2)
        outer_up()

    @pl.when(first & bottom)
    def _():
        pl.semaphore_wait(ok.at[2], 2)
        outer_down()

    @pl.when(jnp.logical_not(top))
    def _():
        pl.semaphore_wait(ok.at[3], rows - 1 - row)

    @pl.loop(row + 1, rows)
    def _(r):
        seeds_to(r)

    def take(slot):
        high[slot], mid[slot], low[slot] = split(slabs[slot, 0:depth, :], 3)

    across_of = seat + 2 - 4 * side + 1
    beside = partner - base + 1
    far = mirror + 1 - 2 * core - base + 1
    take(place)
    arrived(beside)
    take(beside)
    arrived(across_of)
    send(0, across_of, across_of, partner)
    take(across_of)

    for load in loads[3:]:
        load.wait()
    waiting(picks.at[pl.ds(0, rows - 1)], send_sem.at[2], small_sem.at[0]).wait_recv()
    picked = jnp.concatenate([picks[...].reshape(total, 128)] * (params // 128), axis=1)
    chosen = picked == lax.broadcasted_iota(jnp.int32, (total, params), 1)
    viscosity = jnp.sum(jnp.where(chosen, visc_ref[...], 0.0), axis=1, keepdims=True)
    chosen = chosen.astype(jnp.float32)
    coeffs = lax.dot(chosen, coeff_ref[...], precision=lax.Precision.HIGHEST)
    forcing = lax.dot(chosen, force_ref[...], precision=lax.Precision.HIGHEST)

    def speeds_of(now, terms):
        one = product(now, terms[0], LANES)
        two = product(now[: 2 * total], terms[1], LANES)
        three = product(now[:total], terms[2], LANES)
        small = (one[2 * total :] + two[total:]) + three
        return (small + (one[total : 2 * total] + two[:total])) + one[:total]

    now = stack(coeffs, 3)

    def gather(slot):
        speed = speeds_of(now, [t[slot] for t in (high, mid, low)])
        for a in range(2):
            speeds[a, slot] = speed[:, a * cells : (a + 1) * cells]

    gather(place)
    gather(beside)
    gather(across_of)
    outer = (ROW + 1) * core
    arrived(far)
    take(far)
    gather(far)
    scale = jnp.concatenate(
        [
            jnp.broadcast_to(slabs[s + 1, depth : depth + 1, :], (total, cells))
            for s in range(ROW)
        ],
        axis=0,
    )
    early = lax.broadcasted_iota(jnp.int32, (1, cells), 1) < across
    down = lax.broadcasted_iota(jnp.int32, (cells, cells), 0)
    right = lax.broadcasted_iota(jnp.int32, (cells, cells), 1)
    same = (down < across) == (right < across)
    apart = down - right
    apart = jnp.where(apart < 0, apart + across, apart)
    stencil = jnp.where(apart == 1, 8.0, 0.0) - jnp.where(apart == 2, 1.0, 0.0)
    stencil += jnp.where(apart == across - 2, 1.0, 0.0) - jnp.where(apart == across - 1, 8.0, 0.0)
    stencil = jnp.where(same, stencil, 0.0).astype(jnp.bfloat16)

    def cross_slope(f):
        height = f.shape[0]
        sums = product(stack(f, 3), stencil, ROWS)
        return (sums[2 * height :] + sums[height : 2 * height]) + sums[:height]

    def along_slope(f):
        swapped = pltpu.roll(f, across, 1)
        width = f.shape[0] - 2 * total

        def three(g):
            return g[:width], g[total : total + width], g[2 * total :]

        before, here, after = three(swapped)
        step = jnp.where(early, here - before, after - here)
        before, _, after = three(f)
        return (before - after) + 8.0 * step

    damping = viscosity * (1.0 / 144.0)
    inner = ROW * total
    nothing = jnp.zeros((2 * total, cells), jnp.float32)

    def across_part(middle):
        cross = cross_slope(jnp.concatenate(middle, axis=0))
        cross = [cross[:inner], cross[inner:]]
        return cross, cross_slope(jnp.concatenate([scale * f for f in cross], axis=0))

    def change_of(u, parts_across):
        middle = [f[total : total + inner] for f in u]
        along = [along_slope(f) for f in u]
        cross, spread_cross = parts_across
        fields = []
        for a in range(2):
            carried = (scale * (1.0 / 12.0)) * (middle[0] * along[a] + middle[1] * cross[a])
            damped = along_slope(jnp.concatenate([nothing, scale * along[a], nothing], axis=0))
            field = []
            for s in range(ROW + 2):
                f = damped[s * total : (s + 1) * total]
                if 1 <= s <= ROW:
                    at = slice((s - 1) * total, s * total)
                    f = f + spread_cross[a * inner : (a + 1) * inner][at]
                    field.append(carried[at] - damping * f)
                else:
                    field.append(-damping * f)
            fields.append(field)
        parts = [f[s] for s in range(ROW + 2) for f in fields]
        both = stack(jnp.concatenate(parts, axis=1), 2)
        size = (ROW + 2) * depth
        sums = product(both, high[...].reshape(size, -1), ROWS)
        rest = product(both[:total], mid[...].reshape(size, -1), ROWS)
        return (rest + sums[total:]) + sums[:total]

    def inside(u):
        return [f[total : total + inner] for f in u]

    own_part = across_part(
        [speeds[a, 1 : ROW + 1].reshape(inner, cells) for a in range(2)]
    )
    arrived(outer)
    send(0, outer, outer, partner)
    take(outer)
    gather(outer)
    arrived(ROW + 1 - outer)
    take(ROW + 1 - outer)
    gather(ROW + 1 - outer)

    change = change_of([speeds[a].reshape((ROW + 2) * total, cells) for a in range(2)], own_part)
    partial[...] = change
    spread(1, lambda r: partial, lambda d: landed.at[d - 1])
    waiting(landed, send_sem.at[3], small_sem.at[1]).wait_recv()
    coeffs = coeffs + TIME_STEP * (forcing - (change + jnp.sum(landed[...], axis=0)))
    now_ref[...] = coeffs.reshape(rows, own, -1)
    push_ref[...] = forcing.reshape(rows, own, -1)
    terms = [t[...].reshape((ROW + 2) * depth, -1) for t in (high, mid, low)]
    speed = speeds_of(stack(coeffs, 3), terms)
    u = []
    for a in range(2):
        starts = [s * depth + a * cells for s in range(ROW + 2)]
        u.append(jnp.concatenate([speed[:, i : i + cells] for i in starts], axis=0))
    last[...] = change_of(u, across_part(inside(u))).reshape(rows, own, -1)
    spread(2, lambda r: last.at[r], lambda d: last_landed.at[d - 1])
    waiting(last_landed, send_sem.at[4], small_sem.at[2]).wait_recv()
    change = last[row] + jnp.sum(last_landed[...], axis=0)
    out_ref[...] = now_ref[row] + TIME_STEP * (push_ref[row] - change)

    waiting(slabs.at[pl.ds(0, 4)], send_sem.at[0], recv_sem.at[0]).wait_send()

    @pl.when(first | final)
    def _():
        waiting(slabs.at[pl.ds(0, 2)], send_sem.at[1], recv_sem.at[0]).wait_send()

    waiting(picks.at[pl.ds(0, rows - 1)], send_sem.at[2], small_sem.at[0]).wait_send()
    waiting(landed, send_sem.at[3], small_sem.at[1]).wait_send()
    waiting(last_landed, send_sem.at[4], small_sem.at[2]).wait_send()


def shards(modes, cell_weight, seeds, coeff_table, force_table, visc_table):
    components, mode_count, layers, across = modes.shape
    n = lax.axis_size("space")
    rows = n // ROW
    cells = layers * across
    depth = components * cells
    own = seeds.shape[0]
    total = own * rows
    params = coeff_table.shape[0]
    f32, bf16 = jnp.float32, jnp.bfloat16
    return pl.pallas_call(
        functools.partial(kernel, n, across),
        out_shape=pltpu.VMEM((own, mode_count), f32),
        in_specs=[pl.BlockSpec(memory_space=pl.ANY)] * 6,
        out_specs=pl.BlockSpec(memory_space=pltpu.VMEM),
        scratch_shapes=[
            pltpu.VMEM((ROW + 2, depth + TAIL, mode_count), f32),
            pltpu.VMEM((ROW + 2, depth, mode_count), bf16),
            pltpu.VMEM((ROW + 2, depth, mode_count), bf16),
            pltpu.VMEM((ROW + 2, depth, mode_count), bf16),
            pltpu.VMEM((components, ROW + 2, total, cells), f32),
            pltpu.VMEM((layers, across), f32),
            pltpu.SMEM((own,), jnp.int32),
            pltpu.VMEM((1, params), f32),
            pltpu.VMEM((params, mode_count), f32),
            pltpu.VMEM((params, mode_count), f32),
            pltpu.VMEM((rows, own, 128), jnp.int32),
            pltpu.VMEM((total, mode_count), f32),
            pltpu.VMEM((rows - 1, total, mode_count), f32),
            pltpu.VMEM((rows, own, mode_count), f32),
            pltpu.VMEM((rows, own, mode_count), f32),
            pltpu.VMEM((rows, own, mode_count), f32),
            pltpu.VMEM((rows - 1, own, mode_count), f32),
            pltpu.SemaphoreType.DMA((6,)),
            pltpu.SemaphoreType.DMA((5,)),
            pltpu.SemaphoreType.DMA((ROW + 2,)),
            pltpu.SemaphoreType.DMA((3,)),
            pltpu.SemaphoreType.REGULAR((4,)),
        ],
        compiler_params=pltpu.CompilerParams(collective_id=0, has_side_effects=True),
    )(
        modes.transpose(0, 2, 3, 1).reshape(depth, mode_count),
        cell_weight,
        seeds,
        visc_table.reshape(1, -1),
        coeff_table,
        force_table,
    )


def solution(mesh):
    placed = (
        P("groups", None, "space", None),
        P("space", "groups"),
        P(("groups", "space")),
        P(),
        P(),
        P(),
    )
    return jax.shard_map(
        shards, mesh=mesh, in_specs=placed, out_specs=P(("groups", "space"), None), check_vma=False
    )
```

time: 24 us -> 23.2 us (0.967)
  Pallas kernels: 23.3 us -> 22.5 us
    pallas_call x1, Pallas kernels: 23.3 us -> 22.5 us  [shards(): pl.pallas_call(functools.partial(kernel, n, across), out_shape=pltpu.VMEM...]
where the time goes in v1:
time: 23.2 us; the launch traced here: 23.1 us
  Pallas kernels  22.5 us (97%)
  local copies, waits for them, and re-layouts  0.6 us (3%)
    pallas_call x1, Pallas kernels, shards(): pl.pallas_call(functools.partial(kernel, n, across), out_shape=pltpu.VMEM...  22.5 us
    unnamed x1, local copies, waits for them, and re-layouts  0.6 us

profile of v1, /device:TPU:0, one launch (start us, length us, event | category | flops | bytes accessed | tf_op | source)
XLA Modules:
  0.0 23.1 jit_solution(104490303290263723)
XLA Ops:
  0.0 22.5 %shard_map.64 = f32[8,128]{1,0:T(8,128)S(1)} custom-call(f32[256,128]{1,0:T(8,128)} %bitcast.4, f32[2,64]{1,0:T(2,128)} %weight_hbm.1, s32[8]{0:T(128)} %seeds_hbm.1, f32[1,256]{1,0:T(1,128)} %bitcast.5, f32[256,128]{1,0:T(8,128)} %coeff_hbm.1, f32[256,128]{1,0:T(8,128)} %force_hbm.1), custom_call_target="tpu_custom_call" | custom-call | tf_op jit(solution)/shard_map/pallas_call | solution.py:453
  22.5 0.6 %copy.8 = f32[8,128]{1,0:T(8,128)} copy(f32[8,128]{1,0:T(8,128)S(1)} %shard_map.64) | data formatting | bytes 8192

commit v2 on v1

--- a/solution.py
+++ b/solution.py
@@ -345,10 +345,13 @@
     stencil += jnp.where(apart == across - 2, 1.0, 0.0) - jnp.where(apart == across - 1, 8.0, 0.0)
     stencil = jnp.where(same, stencil, 0.0).astype(jnp.bfloat16)
 
-    def cross_slope(f):
+    def cross_slope(f, count):
         height = f.shape[0]
-        sums = product(stack(f, 3), stencil, ROWS)
-        return (sums[2 * height :] + sums[height : 2 * height]) + sums[:height]
+        sums = product(stack(f, count), stencil, ROWS)
+        slope = sums[(count - 1) * height :]
+        for k in reversed(range(count - 1)):
+            slope = slope + sums[k * height : (k + 1) * height]
+        return slope
 
     def along_slope(f):
         swapped = pltpu.roll(f, across, 1)
@@ -367,9 +370,9 @@
     nothing = jnp.zeros((2 * total, cells), jnp.float32)
 
     def across_part(middle):
-        cross = cross_slope(jnp.concatenate(middle, axis=0))
+        cross = cross_slope(jnp.concatenate(middle, axis=0), 3)
         cross = [cross[:inner], cross[inner:]]
-        return cross, cross_slope(jnp.concatenate([scale * f for f in cross], axis=0))
+        return cross, cross_slope(jnp.concatenate([scale * f for f in cross], axis=0), 2)
 
     def change_of(u, parts_across):
         middle = [f[total : total + inner] for f in u]

time: 23.2 us -> 23.2 us (level)
  no operation moved by 1% of the time
where the time goes in v2:
time: 23.2 us; the launch traced here: 23 us
  Pallas kernels  22.4 us (97%)
  local copies, waits for them, and re-layouts  0.6 us (3%)
    pallas_call x1, Pallas kernels, shards(): pl.pallas_call(functools.partial(kernel, n, across), out_shape=pltpu.VMEM...  22.4 us
    unnamed x1, local copies, waits for them, and re-layouts  0.6 us

profile of v2, /device:TPU:0, one launch (start us, length us, event | category | flops | bytes accessed | tf_op | source)
XLA Modules:
  0.0 23.0 jit_solution(7168609584374160732)
XLA Ops:
  0.0 22.4 %shard_map.64 = f32[8,128]{1,0:T(8,128)S(1)} custom-call(f32[256,128]{1,0:T(8,128)} %bitcast.4, f32[2,64]{1,0:T(2,128)} %weight_hbm.1, s32[8]{0:T(128)} %seeds_hbm.1, f32[1,256]{1,0:T(1,128)} %bitcast.5, f32[256,128]{1,0:T(8,128)} %coeff_hbm.1, f32[256,128]{1,0:T(8,128)} %force_hbm.1), custom_call_target="tpu_custom_call" | custom-call | tf_op jit(solution)/shard_map/pallas_call | solution.py:456
  22.4 0.6 %copy.8 = f32[8,128]{1,0:T(8,128)} copy(f32[8,128]{1,0:T(8,128)S(1)} %shard_map.64) | data formatting | bytes 8192
